TPU v7x, 256 devices: a whole 4x4x8 slice. The times are simulated.
256 devices in a mesh: slab: 32 (over z, x), orb: 8 (over y, core).
Axes of the slice: x: 4, y: 4, z: 8, core: 2. Of those that a mesh axis runs over, the one named last changes fastest.
Arguments:
- orbitals: bfloat16 [32, 8, 1, 64, 2304], P(None, 'orb', None, 'slab'), may hold values from -6 to 6
- potential: float32 [64, 2304], P('slab'), may hold values from -1.5 to 0.5
- partners: int32 [32, 8, 1, 2], P('slab', 'orb'), may hold values from 0 to 255, as said below
- pair_valid: int32 [32, 8, 1, 2], P('slab', 'orb'), may hold values from 0 to 1, as said below
Outputs:
- action: bfloat16 [32, 8, 1, 64, 2304], P(None, 'orb', None, 'slab')
Inputs may be any that keep to these rules, and one draw needn't show every extreme that they name: partners names, for orbital number n = (a * 8 + b) + r, an orbital number that differs from n by 1 to 1 along the cyclic order of the 256 orbitals: ahead of n in even slots, behind n in odd slots; a partner may be listed more than once. `pair_valid`: slot 0 of every orbital is used.
All inputs are finite; a program needn't handle non-finite values.
Results may differ from a plain program's by a relative error of at most 0.001.
Values may be sent and summed in bfloat16 or wider, within the bound.
No kernel may reach another device: no remote copies, remote signals or barrier semaphores. Data moves between devices by JAX's collectives and lax.ppermute only.
A program may use at most 64 MiB of HBM per device.

v0:
```python
import math

import jax
import jax.numpy as jnp
from jax import lax
from jax.sharding import PartitionSpec as P

NX = 48
NY = 48
NZ = 64


stencil_weights = (-205.0 / 72.0, 8.0 / 5.0, -1.0 / 5.0, 8.0 / 315.0, -1.0 / 560.0)
screening = 0.11
mixing = 0.25


def with_halo(block, sides, width):
    for axis, dim in sides:
        count = lax.axis_size(axis)
        forward = [(i, i + 1) for i in range(count - 1)]
        forward.append((count - 1, 0))
        backward = [(target, source) for source, target in forward]
        low = lax.ppermute(
            lax.slice_in_dim(block, block.shape[dim] - width, None, axis=dim), axis, forward
        )
        high = lax.ppermute(lax.slice_in_dim(block, 0, width, axis=dim), axis, backward)
        block = jnp.concatenate([low, block, high], axis=dim)
    return block


def squared_wave(length):
    grid = jnp.arange(length, dtype=jnp.int32)
    folded = jnp.minimum(grid, length - grid).astype(jnp.float32)
    return 2.0 * math.pi * folded / length * (2.0 * math.pi * folded / length)


def screened_kernel(depth, rows, cols):
    wave = (
        squared_wave(depth)[:, None, None]
        + squared_wave(rows)[None, :, None]
        + squared_wave(cols)[None, None, :]
    )
    safe = jnp.where(wave > 0, wave, 1.0)
    inner = 4.0 * math.pi / safe * (1.0 - jnp.exp(-safe / (4.0 * screening * screening)))
    return jnp.where(wave > 0, inner, math.pi / (screening * screening))


def hartley(length):
    grid = jnp.arange(length, dtype=jnp.int32)
    phase = grid[:, None] * grid[None, :] % length
    angle = phase.astype(jnp.float32) * (2.0 * math.pi / length)
    return jnp.cos(angle) + jnp.sin(angle)


def rotate_apply(data, matrix, middle):
    product = jnp.dot(
        matrix, data, precision=lax.Precision.HIGHEST, preferred_element_type=jnp.float32
    )
    leading = product.shape[0]
    cubed = product.reshape(leading, middle, product.shape[1] // middle)
    turned = jnp.transpose(cubed, (1, 2, 0))
    return turned.reshape(middle, -1)


def hartley_three(data, tables):
    depth_table, row_table, col_table = tables
    step_one = rotate_apply(data, depth_table, row_table.shape[0])
    step_two = rotate_apply(step_one, row_table, col_table.shape[0])
    return rotate_apply(step_two, col_table, depth_table.shape[0])


def pair_potential(density, tables, kernel):
    return hartley_three(kernel * hartley_three(density, tables), tables)


def lateral_second(field, width_x):
    column = jnp.arange(field.shape[-1], dtype=jnp.int32) % width_x
    total = 2.0 * stencil_weights[0] * field
    for reach in range(1, 5):
        along_y = jnp.roll(field, reach * width_x, -1) + jnp.roll(field, -reach * width_x, -1)
        upper = jnp.where(
            column + reach < width_x,
            jnp.roll(field, -reach, -1),
            jnp.roll(field, width_x - reach, -1),
        )
        lower = jnp.where(
            column >= reach, jnp.roll(field, reach, -1), jnp.roll(field, reach - width_x, -1)
        )
        total = total + stencil_weights[reach] * (along_y + upper + lower)
    return total


def vertical_part(column, depth):
    total = stencil_weights[0] * column[:, :, :, 4 : 4 + depth]
    for reach in range(1, 5):
        above = column[:, :, :, 4 + reach : 4 + reach + depth]
        below = column[:, :, :, 4 - reach : 4 - reach + depth]
        total = total + stencil_weights[reach] * (above + below)
    return total


def planes_of(data):
    return with_halo(data, (("slab", 3),), 2)


def local(orbitals, potential, partners, pair_valid):
    width = orbitals.shape[2]
    depth = orbitals.shape[3]
    count = partners.shape[3]
    values = orbitals.astype(jnp.float32)
    laplace = lateral_second(values, NX)
    near = planes_of(orbitals)
    rims = jnp.concatenate([near[:, :, :, 4:6], near[:, :, :, depth - 2 : depth]], axis=3)
    far = planes_of(rims)
    column = jnp.concatenate([far[:, :, :, 0:2], near, far[:, :, :, 6:8]], axis=3).astype(
        jnp.float32
    )
    laplace = laplace + vertical_part(column, depth)
    owned = lax.all_to_all(orbitals, "slab", split_axis=0, concat_axis=3, tiled=True)
    owned = owned.reshape(width, NZ, NY * NX)
    extended = with_halo(owned, ((("slab", "orb"), 0),), width)
    chain = lax.axis_index("slab") * lax.axis_size("orb") + lax.axis_index("orb")
    total_orbitals = width * lax.axis_size("slab") * lax.axis_size("orb")
    tables = (hartley(NZ), hartley(NY), hartley(NX))
    kernel = screened_kernel(NZ, NY, NX).reshape(NZ, NY * NX) / float(NZ * NY * NX)
    own_lists = partners.reshape(width, count)
    own_flags = pair_valid.reshape(width, count)
    offsets = (own_lists - (chain - 1) * width) % total_orbitals
    weights = own_flags.astype(jnp.float32)

    def pair_turn(slot, accum):
        lister = slot // count
        column_index = slot % count
        partner_row = offsets[lister, column_index]
        weight = weights[lister, column_index]
        first = lax.dynamic_index_in_dim(extended, width + lister, 0, keepdims=False).astype(
            jnp.float32
        )
        second = lax.dynamic_index_in_dim(extended, partner_row, 0, keepdims=False).astype(
            jnp.float32
        )
        field = pair_potential(first * second, tables, kernel) * weight
        accum = accum.at[width + lister].add(field * second)
        accum = accum.at[partner_row].add(field * first)
        return accum

    start = jnp.zeros((3 * width, NZ, NY * NX), jnp.float32)
    partial_value = lax.fori_loop(0, width * count, pair_turn, start)
    outward = jnp.concatenate(
        [partial_value[0:width], partial_value[2 * width : 3 * width]], axis=0
    )
    inward = with_halo(outward, ((("slab", "orb"), 0),), width)
    exchange_term = (
        partial_value[width : 2 * width] + inward[0:width] + inward[3 * width : 4 * width]
    )
    outgoing = -mixing * exchange_term
    outgoing = outgoing.reshape(1, 1, width, NZ, NY * NX)
    returned = lax.all_to_all(outgoing, "slab", split_axis=3, concat_axis=0, tiled=True)
    result = -0.5 * laplace + potential[None, None, None, :, :] * values + returned
    return result.astype(jnp.bfloat16)


def solution(mesh):
    in_specs = (
        P(None, "orb", None, "slab", None),
        P("slab", None),
        P("slab", "orb", None, None),
        P("slab", "orb", None, None),
    )
    out_specs = P(None, "orb", None, "slab", None)
    return jax.shard_map(local, mesh=mesh, in_specs=in_specs, out_specs=out_specs, check_vma=False)
```

profile of v0, /device:TPU:25, one launch (start us, length us, event | category | flops | bytes accessed | tf_op | source)
XLA Modules:
  0.0 220.4 jit_solution(9164087970755809876)
XLA Ops:
  0.0 11.2 %all-to-all-start = ((bf16[32,1,1,2,2304]{4,3,2,1,0:T(2,128)(2,1)}), bf16[32,1,1,2,2304]{4,3,2,1,0:T(2,128)(2,1)S(1)}, u32[]{:S(2)}, u32[]{:S(2)}) async-start(bf16[32,1,1,2,2304]{4,3,2,1,0:T(2,128)(2,1)} %param.10), calls=%async_computation | async-start | bytes 589824 | tf_op jit(solution)/shard_map/all_to_all | solution.py:120
  12.5 3.6 %collective-permute-start.2 = (bf16[32,1,1,2,2304]{4,3,2,1,0:T(2,128)(2,1)}, bf16[32,1,1,2,2304]{4,3,2,1,0:T(2,128)(2,1)}, u32[]{:S(2)}, u32[]{:S(2)}) collective-permute-start(bf16[32,1,1,2,2304]{4,3,2,1,0:T(2,128)(2,1)} %param.10), channel_id=1, source_target_pairs={{8,0},{16,8},{24,16},{32,24},{40,32},{48,40},{56,48},{64,56},{72,6... | collective-permute-start | bytes 884744 | tf_op jit(solution)/shard_map/ppermute | solution.py:27
  16.1 2.6 %fusion.110 = (f32[32,1,1,2,2256]{4,3,2,1,0:T(2,128)}, f32[32,1,1,2,2256]{4,3,2,1,0:T(2,128)}) fusion(bf16[32,1,1,2,2304]{4,3,2,1,0:T(2,128)(2,1)} %param.10), kind=kLoop, calls=%fused_computation.167 | loop fusion | bytes 2310144 | tf_op jit(solution)/shard_map/jit(_roll_static)/slice | solution.py:81
  21.8 1.6 fusion.116
  28.0 1.7 fusion.126
  39.6 1.6 collective-permute-start.5
  43.3 4.7 %collective-permute-done.5 = bf16[1,64,2304]{2,1,0:T(8,128)(2,1)S(1)} collective-permute-done((bf16[1,64,2304]{2,1,0:T(8,128)(2,1)S(1)}, bf16[1,64,2304]{2,1,0:T(8,128)(2,1)S(1)}, u32[]{:S(2)}, u32[]{:S(2)}) %collective-permute-start.5) | collective-permute-done | bytes 294944 | tf_op jit(solution)/shard_map/ppermute | solution.py:27
  50.3 71.5 %while.19 = (s32[]{:T(128)}, f32[3,64,2304]{2,1,0:T(8,128)}, bf16[3,64,2304]{2,1,0:T(8,128)(2,1)}, s32[1,2]{1,0:T(1,128)S(1)}, f32[1,2]{1,0:T(1,128)S(1)}, /*ind...) while((s32[]{:T(128)}, f32[3,64,2304]{2,1,0:T(8,128)}, ...), condition=%wide.region_3.4_spmd.clone.clone, body=%wide.region_0.3_spmd.clone.clone.sunk | while | flops 569837632 | bytes 34825664 | solution.py:149
  64.8 1.9 convolution_bitcast_fusion.10
  86.5 2.7 %fusion.153 = f32[3,64,2304]{2,1,0:T(8,128)} fusion(f32[3,64,2304]{2,1,0:T(8,128)} %get-tuple-element.468, s32[]{:T(128)} %select_n.397, f32[1,64,2304]{2,1,0:T(8,128)S(1)} %mul.842, pred[]{:T(512)} %get-tuple-element.450, bf16[3,64,2304]{2,1,0:T(8,128)(2,1)} %get-tuple-element.484, s32[]{:T(128)} %select_n.400), kind=kLoop, calls=%fused_computation.20.clone.1 | loop fusion | flops 589824 | bytes 2065920 | tf_op jit(solution)/shard_map/while/body/eval_jaxpr/scatter-add | solution.py:144
  89.2 2.7 %fusion.154 = f32[3,64,2304]{2,1,0:T(8,128)} fusion(f32[3,64,2304]{2,1,0:T(8,128)} %fusion.153, s32[]{:T(128)} %select_n.400, f32[1,64,2304]{2,1,0:T(8,128)S(1)} %mul.842, pred[]{:T(512)} %get-tuple-element.451, bf16[3,64,2304]{2,1,0:T(8,128)(2,1)} %get-tuple-element.484, s32[]{:T(128)} %select_n.397), kind=kLoop, calls=%fused_computation.21.clone.1 | loop fusion | flops 589824 | bytes 2065920 | tf_op jit(solution)/shard_map/while/body/eval_jaxpr/scatter-add | solution.py:145
  94.7 1.9 convolution_bitcast_fusion.10
  116.4 2.7 %fusion.153 = f32[3,64,2304]{2,1,0:T(8,128)} fusion(f32[3,64,2304]{2,1,0:T(8,128)} %get-tuple-element.468, s32[]{:T(128)} %select_n.397, f32[1,64,2304]{2,1,0:T(8,128)S(1)} %mul.842, pred[]{:T(512)} %get-tuple-element.450, bf16[3,64,2304]{2,1,0:T(8,128)(2,1)} %get-tuple-element.484, s32[]{:T(128)} %select_n.400), kind=kLoop, calls=%fused_computation.20.clone.1 | loop fusion | flops 589824 | bytes 2065920 | tf_op jit(solution)/shard_map/while/body/eval_jaxpr/scatter-add | solution.py:144
  119.1 2.7 %fusion.154 = f32[3,64,2304]{2,1,0:T(8,128)} fusion(f32[3,64,2304]{2,1,0:T(8,128)} %fusion.153, s32[]{:T(128)} %select_n.400, f32[1,64,2304]{2,1,0:T(8,128)S(1)} %mul.842, pred[]{:T(512)} %get-tuple-element.451, bf16[3,64,2304]{2,1,0:T(8,128)(2,1)} %get-tuple-element.484, s32[]{:T(128)} %select_n.397), kind=kLoop, calls=%fused_computation.21.clone.1 | loop fusion | flops 589824 | bytes 2065920 | tf_op jit(solution)/shard_map/while/body/eval_jaxpr/scatter-add | solution.py:145
  121.9 2.7 %copy.18 = f32[3,64,2304]{2,0,1:T(4,128)S(1)} copy(f32[3,64,2304]{2,1,0:T(8,128)} %get-tuple-element.285) | data formatting | bytes 3538944 | tf_op jit(solution)/shard_map/while | solution.py:149
  127.6 4.8 %collective-permute-done.6 = f32[1,64,2304]{2,0,1:T(1,128)S(1)} collective-permute-done((f32[1,64,2304]{2,0,1:T(1,128)S(1)}, f32[1,64,2304]{2,0,1:T(1,128)S(1)}, u32[]{:S(2)}, u32[]{:S(2)}) %collective-permute-start.6) | collective-permute-done | bytes 589856 | tf_op jit(solution)/shard_map/ppermute | solution.py:24
  132.4 4.7 %collective-permute-done.7 = f32[1,64,2304]{2,0,1:T(1,128)S(1)} collective-permute-done((f32[1,64,2304]{2,0,1:T(1,128)S(1)}, f32[1,64,2304]{2,0,1:T(1,128)S(1)}, u32[]{:S(2)}, u32[]{:S(2)}) %collective-permute-start.7) | collective-permute-done | bytes 589856 | tf_op jit(solution)/shard_map/ppermute | solution.py:27
  137.1 2.0 multiply_bitcast_fusion
  139.1 18.1 %all-to-all-start.1 = ((f32[1,1,1,64,2304]{4,2,1,0,3:T(1,128)}), f32[1,1,1,64,2304]{4,2,1,0,3:T(1,128)S(1)}, u32[]{:S(2)}, u32[]{:S(2)}) async-start(f32[1,1,1,64,2304]{4,2,1,0,3:T(1,128)} %multiply_bitcast_fusion), calls=%async_computation.1 | async-start | bytes 1179648 | tf_op jit(solution)/shard_map/all_to_all | solution.py:159
  161.1 3.6 %collective-permute-start.3 = (bf16[32,1,1,2,2304]{4,3,2,1,0:T(2,128)(2,1)}, bf16[32,1,1,2,2304]{4,3,2,1,0:T(2,128)(2,1)}, u32[]{:S(2)}, u32[]{:S(2)}) collective-permute-start(bf16[32,1,1,2,2304]{4,3,2,1,0:T(2,128)(2,1)} %collective-permute-done.2), channel_id=1, source_target_pairs={{8,0},{16,8},{24,16},{32,24},{40,32},{48,40},{56,48},{64,56},{72,6... | collective-permute-start | bytes 884744 | tf_op jit(solution)/shard_map/ppermute | solution.py:27
  166.0 8.6 %collective-permute-done.1 = bf16[32,1,1,2,2304]{4,3,2,1,0:T(2,128)(2,1)S(1)} collective-permute-done((bf16[32,1,1,2,2304]{4,3,2,1,0:T(2,128)(2,1)}, bf16[32,1,1,2,2304]{4,3,2,1,0:T(2,128)(2,1)S(1)}, u32[]{:S(2)}, u32[]{:S(2)}) %collective-permute-start.1) | collective-permute-done | bytes 294944 | tf_op jit(solution)/shard_map/ppermute | solution.py:24
  174.7 9.2 %concatenate.346 = bf16[32,1,1,10,2304]{4,3,2,1,0:T(8,128)(2,1)S(1)} concatenate(bf16[32,1,1,2,2304]{4,3,2,1,0:T(2,128)(2,1)S(1)} %collective-permute-done.1, bf16[32,1,1,2,2304]{4,3,2,1,0:T(2,128)(2,1)} %collective-permute-done, bf16[32,1,1,2,2304]{4,3,2,1,0:T(2,128)(2,1)S(1)} %copy-done, bf16[32,1,1,2,2304]{4,3,2,1,0:T(2,128)(2,1)} %collective-permute-done.2, ...), dimensions={3} | concatenate | bytes 2949120 | tf_op jit(solution)/shard_map/concatenate | solution.py:116
  183.9 2.7 %convert_element_type.92 = f32[32,1,1,10,2304]{4,3,2,1,0:T(8,128)} convert(bf16[32,1,1,10,2304]{4,3,2,1,0:T(8,128)(2,1)S(1)} %concatenate.346) | non-fusion elementwise | flops 737280 | bytes 4423680 | tf_op jit(solution)/shard_map/convert_element_type | solution.py:116
  186.7 33.3 %fusion.93 = bf16[32,1,1,2,2304]{4,3,2,1,0:T(2,128)(2,1)} fusion(f32[32,1,1,2,2304]{4,1,3,2,0:T(1,128)S(1)} %bitcast.88, f32[32,1,1,10,2304]{4,3,2,1,0:T(8,128)} %convert_element_type.92, f32[32,1,1,2,44]{4,3,2,1,0:T(2,128)} %get-tuple-element.394, f32[32,1,1,2,2260]{4,3,2,1,0:T(2,128)} %get-tuple-element.396, ...), kind=kLoop, calls=%fused_computation.136 | loop fusion | flops 10764288 | bytes 20680704 | tf_op jit(solution)/shard_map/convert_element_type | solution.py:161
  (121 shorter events, 72.4 us)
Async XLA Ops:
  0.0 18.7 %copy-start = (bf16[32,1,1,2,2304]{4,3,2,1,0:T(2,128)(2,1)S(1)}, bf16[32,1,1,2,2304]{4,3,2,1,0:T(2,128)(2,1)}, u32[]{:S(2)}) copy-start(bf16[32,1,1,2,2304]{4,3,2,1,0:T(2,128)(2,1)} %param.10) | copy-start | bytes 884740
  0.0 39.4 %all-to-all-start = ((bf16[32,1,1,2,2304]{4,3,2,1,0:T(2,128)(2,1)}), bf16[32,1,1,2,2304]{4,3,2,1,0:T(2,128)(2,1)S(1)}, u32[]{:S(2)}, u32[]{:S(2)}) async-start(bf16[32,1,1,2,2304]{4,3,2,1,0:T(2,128)(2,1)} %param.10), calls=%async_computation | async-start | bytes 589824 | tf_op jit(solution)/shard_map/all_to_all | solution.py:120
  11.2 148.7 %collective-permute-start = (bf16[32,1,1,2,2304]{4,3,2,1,0:T(2,128)(2,1)}, bf16[32,1,1,2,2304]{4,3,2,1,0:T(2,128)(2,1)}, u32[]{:S(2)}, u32[]{:S(2)}) collective-permute-start(bf16[32,1,1,2,2304]{4,3,2,1,0:T(2,128)(2,1)} %param.10), channel_id=1, source_target_pairs={{0,8},{8,16},{16,24},{24,32},{32,40},{40,48},{48,56},{56,64},{64,7... | collective-permute-start | bytes 884744 | tf_op jit(solution)/shard_map/ppermute | solution.py:24
  12.5 148.6 %collective-permute-start.2 = (bf16[32,1,1,2,2304]{4,3,2,1,0:T(2,128)(2,1)}, bf16[32,1,1,2,2304]{4,3,2,1,0:T(2,128)(2,1)}, u32[]{:S(2)}, u32[]{:S(2)}) collective-permute-start(bf16[32,1,1,2,2304]{4,3,2,1,0:T(2,128)(2,1)} %param.10), channel_id=1, source_target_pairs={{8,0},{16,8},{24,16},{32,24},{40,32},{48,40},{56,48},{64,56},{72,6... | collective-permute-start | bytes 884744 | tf_op jit(solution)/shard_map/ppermute | solution.py:27
  31.2 6.6 %copy-start.8 = (s32[1,1,1,2]{3,2,1,0:T(1,128)S(1)}, s32[1,1,1,2]{3,2,1,0:T(1,128)}, u32[]{:S(2)}) copy-start(s32[1,1,1,2]{3,2,1,0:T(1,128)} %param.13) | copy-start | bytes 28
  31.2 6.6 %copy-start.9 = (s32[1,1,1,2]{3,2,1,0:T(1,128)S(1)}, s32[1,1,1,2]{3,2,1,0:T(1,128)}, u32[]{:S(2)}) copy-start(s32[1,1,1,2]{3,2,1,0:T(1,128)} %param.12) | copy-start | bytes 28
  39.5 3.8 %collective-permute-start.4 = (bf16[1,64,2304]{2,1,0:T(8,128)(2,1)S(1)}, bf16[1,64,2304]{2,1,0:T(8,128)(2,1)S(1)}, u32[]{:S(2)}, u32[]{:S(2)}) collective-permute-start(bf16[1,64,2304]{2,1,0:T(8,128)(2,1)S(1)} %reshape.1102), channel_id=1, source_target_pairs={{0,1},{1,2},{2,3},{3,4},{4,5},{5,6},{6,7},{7,8},{8,9},{9,10},{10,1... | collective-permute-start | bytes 884744 | tf_op jit(solution)/shard_map/ppermute | solution.py:24
  39.6 8.3 %collective-permute-start.5 = (bf16[1,64,2304]{2,1,0:T(8,128)(2,1)S(1)}, bf16[1,64,2304]{2,1,0:T(8,128)(2,1)S(1)}, u32[]{:S(2)}, u32[]{:S(2)}) collective-permute-start(bf16[1,64,2304]{2,1,0:T(8,128)(2,1)S(1)} %reshape.1102), channel_id=1, source_target_pairs={{1,0},{2,1},{3,2},{4,3},{5,4},{6,5},{7,6},{8,7},{9,8},{10,9},{11,1... | collective-permute-start | bytes 884744 | tf_op jit(solution)/shard_map/ppermute | solution.py:27
  41.9 8.4 %copy-start.7 = (s32[3]{0:T(128)S(1)}, s32[3]{0:T(128)}, u32[]{:S(2)}) copy-start(s32[3]{0:T(128)} %constant.257.clone.3) | copy-start | bytes 40
  74.8 1.2 copy-start.1
  104.7 1.2 copy-start.1
  125.5 6.9 %collective-permute-start.6 = (f32[1,64,2304]{2,0,1:T(1,128)S(1)}, f32[1,64,2304]{2,0,1:T(1,128)S(1)}, u32[]{:S(2)}, u32[]{:S(2)}) collective-permute-start(f32[1,64,2304]{2,0,1:T(1,128)S(1)} %get-tuple-element.347), channel_id=1, source_target_pairs={{0,1},{1,2},{2,3},{3,4},{4,5},{5,6},{6,7},{7,8},{8,9},{9,10},{10,1... | collective-permute-start | bytes 1769480 | tf_op jit(solution)/shard_map/ppermute | solution.py:24
  125.6 11.5 %collective-permute-start.7 = (f32[1,64,2304]{2,0,1:T(1,128)S(1)}, f32[1,64,2304]{2,0,1:T(1,128)S(1)}, u32[]{:S(2)}, u32[]{:S(2)}) collective-permute-start(f32[1,64,2304]{2,0,1:T(1,128)S(1)} %get-tuple-element.348), channel_id=1, source_target_pairs={{1,0},{2,1},{3,2},{4,3},{5,4},{6,5},{7,6},{8,7},{9,8},{10,9},{11,1... | collective-permute-start | bytes 1769480 | tf_op jit(solution)/shard_map/ppermute | solution.py:27
  139.1 47.6 %all-to-all-start.1 = ((f32[1,1,1,64,2304]{4,2,1,0,3:T(1,128)}), f32[1,1,1,64,2304]{4,2,1,0,3:T(1,128)S(1)}, u32[]{:S(2)}, u32[]{:S(2)}) async-start(f32[1,1,1,64,2304]{4,2,1,0,3:T(1,128)} %multiply_bitcast_fusion), calls=%async_computation.1 | async-start | bytes 1179648 | tf_op jit(solution)/shard_map/all_to_all | solution.py:159
  159.9 14.8 %collective-permute-start.1 = (bf16[32,1,1,2,2304]{4,3,2,1,0:T(2,128)(2,1)}, bf16[32,1,1,2,2304]{4,3,2,1,0:T(2,128)(2,1)S(1)}, u32[]{:S(2)}, u32[]{:S(2)}) collective-permute-start(bf16[32,1,1,2,2304]{4,3,2,1,0:T(2,128)(2,1)} %collective-permute-done), channel_id=1, source_target_pairs={{0,8},{8,16},{16,24},{24,32},{32,40},{40,48},{48,56},{56,64},{64,7... | collective-permute-start | bytes 884744 | tf_op jit(solution)/shard_map/ppermute | solution.py:24
  161.1 13.6 %collective-permute-start.3 = (bf16[32,1,1,2,2304]{4,3,2,1,0:T(2,128)(2,1)}, bf16[32,1,1,2,2304]{4,3,2,1,0:T(2,128)(2,1)}, u32[]{:S(2)}, u32[]{:S(2)}) collective-permute-start(bf16[32,1,1,2,2304]{4,3,2,1,0:T(2,128)(2,1)} %collective-permute-done.2), channel_id=1, source_target_pairs={{8,0},{16,8},{24,16},{32,24},{40,32},{48,40},{56,48},{64,56},{72,6... | collective-permute-start | bytes 884744 | tf_op jit(solution)/shard_map/ppermute | solution.py:27
  183.9 2.8 %copy-start.2 = (f32[32,1,1,2,144]{4,3,2,1,0:T(2,128)S(1)}, f32[32,1,1,2,144]{4,3,2,1,0:T(2,128)}, u32[]{:S(2)}) copy-start(f32[32,1,1,2,144]{4,3,2,1,0:T(2,128)} %get-tuple-element.373) | copy-start | bytes 110596
  183.9 2.8 %copy-start.3 = (f32[32,1,1,2,144]{4,3,2,1,0:T(2,128)S(1)}, f32[32,1,1,2,144]{4,3,2,1,0:T(2,128)}, u32[]{:S(2)}) copy-start(f32[32,1,1,2,144]{4,3,2,1,0:T(2,128)} %get-tuple-element.374) | copy-start | bytes 110596
  183.9 2.8 %copy-start.4 = (f32[32,1,1,2,192]{4,3,2,1,0:T(2,128)S(1)}, f32[32,1,1,2,192]{4,3,2,1,0:T(2,128)}, u32[]{:S(2)}) copy-start(f32[32,1,1,2,192]{4,3,2,1,0:T(2,128)} %get-tuple-element.385) | copy-start | bytes 147460
  183.9 2.8 %copy-start.5 = (f32[32,1,1,2,192]{4,3,2,1,0:T(2,128)S(1)}, f32[32,1,1,2,192]{4,3,2,1,0:T(2,128)}, u32[]{:S(2)}) copy-start(f32[32,1,1,2,192]{4,3,2,1,0:T(2,128)} %get-tuple-element.386) | copy-start | bytes 147460
  183.9 2.8 %copy-start.6 = (f32[32,1,1,2,48]{4,3,2,1,0:T(2,128)S(1)}, f32[32,1,1,2,48]{4,3,2,1,0:T(2,128)}, u32[]{:S(2)}) copy-start(f32[32,1,1,2,48]{4,3,2,1,0:T(2,128)} %get-tuple-element.349) | copy-start | bytes 36868
where the time goes:
time: 224 us; the launch traced here: 220 us
  local copies, waits for them, and re-layouts  72.1 us (32%)
  other arithmetic  52.8 us (24%)
  starting transfers between devices  41.1 us (18%)
  waiting for transfers between devices  24.2 us (11%)
  loops' own time  16.2 us (7%)
  matrix products  13.3 us (6%)
    convert_element_type x1, other arithmetic, local(): return result.astype(jnp.bfloat16)  33.3 us
    all_to_all x1, starting transfers between devices, local(): lax.all_to_all(outgoing, 'slab', split_axis=3, concat_axis=0, tiled=True)  18.1 us
    another operation x1, loops' own time, local(): partial_value = lax.fori_loop(0, width * count, pair_turn, start)  16.2 us
    ppermute x4, waiting for transfers between devices, with_halo(): lax.ppermute(lax.slice_in_dim(block, block.shape[dim] - width, None, axis...  14.8 us
    dot_general x12, matrix products, rotate_apply(): jnp.dot(matrix, data, precision=lax.Precision.HIGHEST, preferred_element_...  13.3 us
    all_to_all x1, starting transfers between devices, local(): lax.all_to_all(orbitals, 'slab', split_axis=0, concat_axis=3, tiled=True)  11.2 us
    slice x8, local copies, waits for them, and re-layouts, lateral_second(): jnp.roll(field, reach * width_x, -1) + jnp.roll(field, -reach * width_x, -1)  10.1 us
    ppermute x4, waiting for transfers between devices, with_halo(): lax.ppermute(lax.slice_in_dim(block, 0, width, axis=dim), axis, backward)  9.35 us
  transfers between devices with their start and end apart: 10, of which 5 were waited for; matrix products, arithmetic and copies ran while one was open for 48% of the time, Pallas kernels for 0%

commit v1 on v0

v1 whole, which is shorter than its diff:
```python
import math

import jax
import jax.numpy as jnp
import numpy as np
from jax import lax
from jax.experimental import pallas as pl
from jax.experimental.pallas import tpu as pltpu
from jax.sharding import PartitionSpec as P

NX = 48
NY = 48
NZ = 64
NYX = NY * NX
LANES = 128
CHUNKS = NYX // LANES
GROUP = 384
REACH_LANES = 256
WINDOW = GROUP + 2 * REACH_LANES

stencil_weights = (-205.0 / 72.0, 8.0 / 5.0, -1.0 / 5.0, 8.0 / 315.0, -1.0 / 560.0)
screening = 0.11
mixing = 0.25

BF16 = jnp.bfloat16
F32 = jnp.float32


def split_table(table):
    wide = np.asarray(table, np.float32)
    high = wide.astype(jnp.bfloat16)
    low = (np.asarray(table, np.float64) - high.astype(np.float64)).astype(jnp.bfloat16)
    return high, low


def hartley(length):
    grid = np.arange(length)
    angle = (grid[:, None] * grid[None, :] % length) * (2.0 * np.pi / length)
    return np.cos(angle) + np.sin(angle)


def squared_wave(length):
    grid = np.arange(length)
    folded = np.minimum(grid, length - grid).astype(np.float64)
    return (2.0 * np.pi * folded / length) ** 2


def kernel_table():
    wave = (
        squared_wave(NX)[:, None, None]
        + squared_wave(NY)[None, :, None]
        + squared_wave(NZ)[None, None, :]
    )
    safe = np.where(wave > 0, wave, 1.0)
    inner = 4.0 * np.pi / safe * (1.0 - np.exp(-safe / (4.0 * screening * screening)))
    full = np.where(wave > 0, inner, np.pi / (screening * screening)) / (NZ * NYX)
    full = full.reshape(NX * NY, NZ)
    return np.concatenate([full, full], axis=1).astype(np.float32)


def depth_table():
    pair = np.kron(np.eye(2), hartley(NZ))
    high, low = split_table(pair)
    top = np.concatenate([high, low], axis=1)
    bottom = np.concatenate([high, np.zeros_like(low)], axis=1)
    return np.concatenate([top, bottom], axis=0)


def side_table():
    high, low = split_table(hartley(NX))
    return np.concatenate([high, high, low], axis=1)


def second_difference(length):
    table = np.zeros((length, length))
    for spot in range(length):
        table[spot, spot] += stencil_weights[0]
        for reach in range(1, 5):
            table[spot, (spot + reach) % length] += stencil_weights[reach]
            table[spot, (spot - reach) % length] += stencil_weights[reach]
    return table


def vertical_table():
    high, low = split_table(-0.5 * second_difference(NZ))
    return np.concatenate([high, low], axis=1)


def lateral_table():
    table = np.zeros((WINDOW, GROUP))
    along_x = second_difference(NX)
    for lane in range(GROUP):
        row, col = divmod(lane, NX)
        for other in range(NX):
            table[REACH_LANES + row * NX + other, lane] += along_x[col, other]
        table[REACH_LANES + lane, lane] += stencil_weights[0]
        for reach in range(1, 5):
            table[REACH_LANES + lane + reach * NX, lane] += stencil_weights[reach]
            table[REACH_LANES + lane - reach * NX, lane] += stencil_weights[reach]
    high, low = split_table(-0.5 * table)
    return np.concatenate([high, low], axis=0)


def halves(value):
    high = value.astype(BF16)
    low = (value - high.astype(F32)).astype(BF16)
    return high, low


def depth_turn(value, table):
    high, low = halves(value)
    both = jnp.dot(
        jnp.concatenate([high, low], axis=1), table, preferred_element_type=F32
    )
    return both[:, :LANES] + both[:, LANES:]


def side_turn(value, table):
    high, low = halves(value)
    return jnp.dot(
        table, jnp.concatenate([high, low, high], axis=0), preferred_element_type=F32
    )


def owner_kernel(
    flags, ahead_flags, own, ahead, behind, depth_t, side_t, wave_t, vert_t, out, work
):
    w_ahead = (flags[0, 0] + ahead_flags[0, 1]).astype(F32) * (-mixing)
    w_behind = (flags[0, 1] + 1).astype(F32) * (-mixing)
    depth = depth_t[...]
    side = side_t[...]
    vert = vert_t[...]

    for chunk in range(CHUNKS):
        cols = slice(chunk * LANES, (chunk + 1) * LANES)
        mine = own[:, cols].astype(F32)
        density = jnp.concatenate(
            [mine * ahead[:, cols].astype(F32), mine * behind[:, cols].astype(F32)], axis=0
        )
        work[cols, :] = depth_turn(density.T, depth)

    def along_x(step):
        first = slice(2 * step * NX, (2 * step + 1) * NX)
        second = slice((2 * step + 1) * NX, (2 * step + 2) * NX)
        turned = side_turn(jnp.concatenate([work[first, :], work[second, :]], axis=1), side)
        work[first, :] = turned[:, :LANES]
        work[second, :] = turned[:, LANES:]

    for step in range(NY // 2):
        along_x(step)
    for step in range(NX // 2):
        first = pl.ds(2 * step, NY, stride=NX)
        second = pl.ds(2 * step + 1, NY, stride=NX)
        turned = side_turn(jnp.concatenate([work[first, :], work[second, :]], axis=1), side)
        factor = jnp.concatenate(
            [
                wave_t[2 * step * NY : (2 * step + 1) * NY, :],
                wave_t[(2 * step + 1) * NY : (2 * step + 2) * NY, :],
            ],
            axis=1,
        )
        turned = side_turn(turned * factor, side)
        work[first, :] = turned[:, :LANES]
        work[second, :] = turned[:, LANES:]
    for step in range(NY // 2):
        along_x(step)

    for chunk in range(CHUNKS):
        cols = slice(chunk * LANES, (chunk + 1) * LANES)
        pots = depth_turn(work[cols, :], depth).T
        mine = own[:, cols]
        term = jnp.dot(vert, jnp.concatenate([mine, mine], axis=0), preferred_element_type=F32)
        term = term + w_ahead * (pots[:NZ] * ahead[:, cols].astype(F32))
        term = term + w_behind * (pots[NZ:] * behind[:, cols].astype(F32))
        high, low = halves(term)
        out[:, cols] = high
        out[:, NYX + chunk * LANES : NYX + (chunk + 1) * LANES] = low


def slab_kernel(planes, potential, lateral_t, out):
    rows = planes.shape[0]
    parity = lax.broadcasted_iota(jnp.int32, (8, GROUP), 0) % 2
    for start in range(0, NYX, GROUP):
        cols = slice(start, start + GROUP)
        pieces = []
        for lane in range(start - REACH_LANES, start + GROUP + REACH_LANES, LANES):
            at = lane % NYX
            pieces.append(planes[:, at : at + LANES])
        window = jnp.concatenate(pieces + pieces, axis=1)
        term = jnp.dot(window, lateral_t[...], preferred_element_type=F32)
        level = jnp.where(
            parity == 0,
            jnp.broadcast_to(potential[0:1, cols], (8, GROUP)),
            jnp.broadcast_to(potential[1:2, cols], (8, GROUP)),
        )
        level = jnp.concatenate([level] * (rows // 8), axis=0)
        out[:, cols] = term + level * planes[:, cols].astype(F32)


def final_kernel(base, returned, out):
    out[...] = (
        base[...] + returned[:, :NYX].astype(F32) + returned[:, NYX:].astype(F32)
    ).astype(BF16)


def vmem():
    return pl.BlockSpec(memory_space=pltpu.VMEM)


def smem():
    return pl.BlockSpec(memory_space=pltpu.SMEM)


def local(orbitals, potential, partners, pair_valid):
    count = lax.axis_size("slab")
    total = count * lax.axis_size("orb")
    to_behind = [((i + 1) % total, i) for i in range(total)]
    to_ahead = [(i, (i + 1) % total) for i in range(total)]
    chain = ("slab", "orb")
    flags = pair_valid.reshape(1, 2)
    ahead_flags = lax.ppermute(flags, chain, to_behind)
    planes = orbitals.reshape(count, 2, NYX)
    own = lax.all_to_all(planes, "slab", split_axis=0, concat_axis=0, tiled=True)
    own = own.reshape(NZ, NYX)
    ahead = lax.ppermute(own, chain, to_behind)
    behind = lax.ppermute(own, chain, to_ahead)

    base = pl.pallas_call(
        slab_kernel,
        out_shape=jax.ShapeDtypeStruct((2 * count, NYX), F32),
        in_specs=[vmem()] * 3,
        out_specs=vmem(),
        name="slab_part",
    )(planes.reshape(2 * count, NYX), potential, jnp.asarray(lateral_table()))

    terms = pl.pallas_call(
        owner_kernel,
        out_shape=jax.ShapeDtypeStruct((NZ, 2 * NYX), BF16),
        in_specs=[smem()] * 2 + [vmem()] * 7,
        out_specs=vmem(),
        scratch_shapes=[pltpu.VMEM((NYX, LANES), F32)],
        name="owner_part",
    )(
        flags,
        ahead_flags,
        own,
        ahead,
        behind,
        jnp.asarray(depth_table()),
        jnp.asarray(side_table()),
        jnp.asarray(kernel_table()),
        jnp.asarray(vertical_table()),
    )
    returned = lax.all_to_all(
        terms.reshape(count, 2, 2 * NYX), "slab", split_axis=0, concat_axis=0, tiled=True
    )
    result = pl.pallas_call(
        final_kernel,
        out_shape=jax.ShapeDtypeStruct((2 * count, NYX), BF16),
        in_specs=[vmem()] * 2,
        out_specs=vmem(),
        name="join_part",
    )(base, returned.reshape(2 * count, 2 * NYX))
    return result.reshape(orbitals.shape)


def solution(mesh):
    in_specs = (
        P(None, "orb", None, "slab", None),
        P("slab", None),
        P("slab", "orb", None, None),
        P("slab", "orb", None, None),
    )
    out_specs = P(None, "orb", None, "slab", None)
    return jax.shard_map(local, mesh=mesh, in_specs=in_specs, out_specs=out_specs, check_vma=False)
```

time: 224 us -> 70.3 us (0.31); the launches traced: 220 us -> 69.8 us
  local copies, waits for them, and re-layouts: 72.1 us -> 7.38 us
  other arithmetic: 52.8 us -> 0 us
  starting transfers between devices: 41.1 us -> 14.4 us
  blocking collectives: 0 us -> 23 us
  loops' own time: 16.2 us -> 0 us
  matrix products: 13.3 us -> 0 us
  Pallas kernels: 0 us -> 10.7 us
  waiting for transfers between devices: 24.2 us -> 14.2 us
    convert_element_type x3 -> x0, other arithmetic: 36 us -> none  [the longest x1 33.3 us: local(): return result.astype(jnp.bfloat16)]
    slice x25 -> x0, local copies, waits for them, and re-layouts: 29.1 us -> none  [the longest x8 10.1 us: lateral_second(): jnp.roll(field, reach * width_x, -1) + jnp.roll(field, -reach * width_x, -1)]
    all_to_all x0 -> x1, blocking collectives: none -> 23 us  [local(): lax.all_to_all(planes, 'slab', split_axis=0, concat_axis=0, tiled=True)]
    ppermute x8 -> x3, waiting for transfers between devices: 24.2 us -> 5.24 us  [the longest x1 5.23 us: local(): ahead_flags = lax.ppermute(flags, chain, to_behind)]
    all_to_all x2 -> x1, starting transfers between devices: 29.2 us -> 10.4 us  [local(): lax.all_to_all(terms.reshape(count, 2, 2 * NYX), 'slab', split_axis=0, co...]
    another operation x1 -> x0, loops' own time: 16.2 us -> none  [local(): partial_value = lax.fori_loop(0, width * count, pair_turn, start)]
    dot_general x12 -> x0, matrix products: 13.3 us -> none  [rotate_apply(): jnp.dot(matrix, data, precision=lax.Precision.HIGHEST, preferred_element_...]
    reshape x21 -> x4, local copies, waits for them, and re-layouts: 16.1 us -> 5.1 us  [the longest x1 2.16 us: local(): terms.reshape(count, 2, 2 * NYX)]
  transfers between devices with their start and end apart: 10 -> 4, of which waited for: 5 -> 2; matrix products, arithmetic and copies ran while one was open for 48% -> 1% of each run, Pallas kernels for 0% -> 5%
where the time goes in v1:
time: 70.3 us; the launch traced here: 69.8 us
  blocking collectives  23 us (33%)
  starting transfers between devices  14.4 us (20%)
  waiting for transfers between devices  14.2 us (20%)
  Pallas kernels  10.7 us (15%)
  local copies, waits for them, and re-layouts  7.38 us (10%)
    all_to_all x1, blocking collectives, local(): lax.all_to_all(planes, 'slab', split_axis=0, concat_axis=0, tiled=True)  23 us
    all_to_all x1, starting transfers between devices, local(): lax.all_to_all(terms.reshape(count, 2, 2 * NYX), 'slab', split_axis=0, co...  10.4 us
    all_to_all x1, waiting for transfers between devices, local(): lax.all_to_all(terms.reshape(count, 2, 2 * NYX), 'slab', split_axis=0, co...  8.99 us
    ppermute x1, waiting for transfers between devices, local(): ahead_flags = lax.ppermute(flags, chain, to_behind)  5.23 us
    pallas_call x1, Pallas kernels, local(): pl.pallas_call(owner_kernel, out_shape=jax.ShapeDtypeStruct((NZ, 2 * NYX)...  5.06 us
    pallas_call x1, Pallas kernels, local(): pl.pallas_call(slab_kernel, out_shape=jax.ShapeDtypeStruct((2 * count, NY...  3.6 us
    ppermute x1, starting transfers between devices, local(): ahead = lax.ppermute(own, chain, to_behind)  2.3 us
    reshape x1, local copies, waits for them, and re-layouts, local(): terms.reshape(count, 2, 2 * NYX)  2.16 us
  transfers between devices with their start and end apart: 4, of which 2 were waited for; matrix products, arithmetic and copies ran while one was open for 1% of the time, Pallas kernels for 5%

profile of v1, /device:TPU:25, one launch (start us, length us, event | category | flops | bytes accessed | tf_op | source)
XLA Modules:
  0.0 69.8 jit_solution(15724235101353777158)
XLA Ops:
  0.0 23.0 %all_to_all.10 = bf16[32,2,2304]{2,1,0:T(2,128)(2,1)S(1)} all-to-all(bf16[32,2,2304]{2,1,0:T(2,128)(2,1)} %bitcast.3), channel_id=1, replica_groups=mesh['slab'=32,'orb'=8] {'slab'}, dimensions={0} | all-to-all | bytes 589824 | tf_op jit(solution)/shard_map/all_to_all | solution.py:223
  23.0 0.1 reshape.20.own
  23.2 0.0 copy-start
  23.2 2.3 %collective-permute-start.1 = (bf16[64,2304]{1,0:T(8,128)(2,1)S(1)}, bf16[64,2304]{1,0:T(8,128)(2,1)S(1)}, u32[]{:S(2)}, u32[]{:S(2)}) collective-permute-start(bf16[64,2304]{1,0:T(8,128)(2,1)S(1)} %reshape.20.own), channel_id=1, source_target_pairs={{1,0},{2,1},{3,2},{4,3},{5,4},{6,5},{7,6},{8,7},{9,8},{10,9},{11,1... | collective-permute-start | bytes 884744 | tf_op jit(solution)/shard_map/ppermute | solution.py:225
  25.5 1.6 %collective-permute-start.2 = (bf16[64,2304]{1,0:T(8,128)(2,1)S(1)}, bf16[64,2304]{1,0:T(8,128)(2,1)S(1)}, u32[]{:S(2)}, u32[]{:S(2)}) collective-permute-start(bf16[64,2304]{1,0:T(8,128)(2,1)S(1)} %reshape.20.own), channel_id=1, source_target_pairs={{0,1},{1,2},{2,3},{3,4},{4,5},{5,6},{6,7},{7,8},{8,9},{9,10},{10,1... | collective-permute-start | bytes 884744 | tf_op jit(solution)/shard_map/ppermute | solution.py:226
  27.1 0.0 collective-permute-start
  27.1 5.2 %collective-permute-done.ahead_flags = s32[1,2]{1,0:T(1,128)S(1)} collective-permute-done((s32[1,2]{1,0:T(1,128)}, s32[1,2]{1,0:T(1,128)S(1)}, u32[]{:S(2)}, u32[]{:S(2)}) %collective-permute-start) | collective-permute-done | bytes 40 | tf_op jit(solution)/shard_map/ppermute | solution.py:221
  32.3 0.0 copy-start.4
  32.3 0.0 collective-permute-done.1.ahead
  32.4 0.0 collective-permute-done.2.behind
  32.4 0.0 copy-done
  32.4 0.6 copy-done.4
  32.9 0.2 copy-done.2
  33.1 0.7 %copy-done.3 = bf16[64,2304]{1,0:T(8,128)(2,1)} copy-done((bf16[64,2304]{1,0:T(8,128)(2,1)}, bf16[64,2304]{1,0:T(8,128)(2,1)S(1)}, u32[]{:S(2)}) %copy-start.3) | copy-done | bytes 294936
  33.8 5.1 %owner_part.1 = bf16[64,4608]{1,0:T(8,128)(2,1)} custom-call(s32[1,2]{1,0:T(1,128)} %bitcast.5, s32[1,2]{1,0:T(1,128)} %copy-done.4, bf16[64,2304]{1,0:T(8,128)(2,1)} %copy-done, bf16[64,2304]{1,0:T(8,128)(2,1)} %copy-done.2, bf16[64,2304]{1,0:T(8,128)(2,1)} %copy-done.3, bf16[256,256]{1,0:T(8,128)(2,1)} %constant.11.clone.depth_t, ...), custom_call_target="tpu_custom_call" | custom-call | tf_op jit(solution)/shard_map/owner_part/pallas_call | solution.py:236
  38.9 2.2 %reshape.21 = bf16[32,2,4608]{2,1,0:T(2,128)(2,1)} reshape(bf16[64,4608]{1,0:T(8,128)(2,1)} %owner_part.1) | data formatting | bytes 1179648 | tf_op jit(solution)/shard_map/reshape | solution.py:255
  41.0 10.4 %all-to-all-start.1 = ((bf16[32,2,4608]{2,1,0:T(2,128)(2,1)}), bf16[32,2,4608]{2,1,0:T(2,128)(2,1)S(1)}, u32[]{:S(2)}, u32[]{:S(2)}) async-start(bf16[32,2,4608]{2,1,0:T(2,128)(2,1)} %reshape.21), calls=%async_computation.1 | async-start | bytes 1179648 | tf_op jit(solution)/shard_map/all_to_all | solution.py:254
  51.5 0.0 copy-done.1
  51.5 0.8 %reshape_reshape.3.planes = bf16[64,2304]{1,0:T(8,128)(2,1)} reshape(bf16[32,1,1,2,2304]{4,3,2,1,0:T(2,128)(2,1)S(1)} %copy-done.1) | data formatting | bytes 589824 | tf_op jit(solution)/shard_map/reshape;reshape | solution.py:234
  52.3 3.6 %slab_part.1.base = f32[64,2304]{1,0:T(8,128)} custom-call(bf16[64,2304]{1,0:T(8,128)(2,1)} %reshape_reshape.3.planes, f32[2,2304]{1,0:T(2,128)} %potential.1, bf16[1792,384]{1,0:T(8,128)(2,1)} %constant.10.clone.lateral_t), custom_call_target="tpu_custom_call" | custom-call | tf_op jit(solution)/shard_map/slab_part/pallas_call | solution.py:228
  55.9 9.0 %all-to-all-done.1 = bf16[32,2,4608]{2,1,0:T(2,128)(2,1)S(1)} async-done(((bf16[32,2,4608]{2,1,0:T(2,128)(2,1)}), bf16[32,2,4608]{2,1,0:T(2,128)(2,1)S(1)}, u32[]{:S(2)}, u32[]{:S(2)}) %all-to-all-start.1) | async-done | bytes 589856 | tf_op jit(solution)/shard_map/all_to_all | solution.py:254
  64.9 1.0 %reshape.22.returned = bf16[64,4608]{1,0:T(8,128)(2,1)} reshape(bf16[32,2,4608]{2,1,0:T(2,128)(2,1)S(1)} %all-to-all-done.1) | data formatting | bytes 1179648 | tf_op jit(solution)/shard_map/reshape | solution.py:263
  65.9 2.1 %join_part.1 = bf16[64,2304]{1,0:T(8,128)(2,1)} custom-call(f32[64,2304]{1,0:T(8,128)} %slab_part.1.base, bf16[64,4608]{1,0:T(8,128)(2,1)} %reshape.22.returned), custom_call_target="tpu_custom_call" | custom-call | tf_op jit(solution)/shard_map/join_part/pallas_call | solution.py:257
  68.0 1.8 %reshape.23 = bf16[32,1,1,2,2304]{4,3,0,2,1:T(2,128)(2,1)} reshape(bf16[64,2304]{1,0:T(8,128)(2,1)} %join_part.1) | data formatting | bytes 589824 | tf_op jit(solution)/shard_map/reshape | solution.py:264
  (3 shorter events, 0.0 us)
Async XLA Ops:
  23.2 9.2 %copy-start = (bf16[64,2304]{1,0:T(8,128)(2,1)}, bf16[64,2304]{1,0:T(8,128)(2,1)S(1)}, u32[]{:S(2)}) copy-start(bf16[64,2304]{1,0:T(8,128)(2,1)S(1)} %reshape.20.own) | copy-start | bytes 884740
  23.2 9.2 %collective-permute-start.1 = (bf16[64,2304]{1,0:T(8,128)(2,1)S(1)}, bf16[64,2304]{1,0:T(8,128)(2,1)S(1)}, u32[]{:S(2)}, u32[]{:S(2)}) collective-permute-start(bf16[64,2304]{1,0:T(8,128)(2,1)S(1)} %reshape.20.own), channel_id=1, source_target_pairs={{1,0},{2,1},{3,2},{4,3},{5,4},{6,5},{7,6},{8,7},{9,8},{10,9},{11,1... | collective-permute-start | bytes 884744 | tf_op jit(solution)/shard_map/ppermute | solution.py:225
  25.5 6.9 %collective-permute-start.2 = (bf16[64,2304]{1,0:T(8,128)(2,1)S(1)}, bf16[64,2304]{1,0:T(8,128)(2,1)S(1)}, u32[]{:S(2)}, u32[]{:S(2)}) collective-permute-start(bf16[64,2304]{1,0:T(8,128)(2,1)S(1)} %reshape.20.own), channel_id=1, source_target_pairs={{0,1},{1,2},{2,3},{3,4},{4,5},{5,6},{6,7},{7,8},{8,9},{9,10},{10,1... | collective-permute-start | bytes 884744 | tf_op jit(solution)/shard_map/ppermute | solution.py:226
  27.1 5.2 %collective-permute-start = (s32[1,2]{1,0:T(1,128)}, s32[1,2]{1,0:T(1,128)S(1)}, u32[]{:S(2)}, u32[]{:S(2)}) collective-permute-start(s32[1,2]{1,0:T(1,128)} %bitcast.4), channel_id=1, source_target_pairs={{1,0},{2,1},{3,2},{4,3},{5,4},{6,5},{7,6},{8,7},{9,8},{10,9},{11,1... | collective-permute-start | bytes 32 | tf_op jit(solution)/shard_map/ppermute | solution.py:221
  32.3 0.6 copy-start.4
  32.4 0.7 %copy-start.2 = (bf16[64,2304]{1,0:T(8,128)(2,1)}, bf16[64,2304]{1,0:T(8,128)(2,1)S(1)}, u32[]{:S(2)}) copy-start(bf16[64,2304]{1,0:T(8,128)(2,1)S(1)} %collective-permute-done.1.ahead) | copy-start | bytes 884740
  33.1 0.7 %copy-start.3 = (bf16[64,2304]{1,0:T(8,128)(2,1)}, bf16[64,2304]{1,0:T(8,128)(2,1)S(1)}, u32[]{:S(2)}) copy-start(bf16[64,2304]{1,0:T(8,128)(2,1)S(1)} %collective-permute-done.2.behind) | copy-start | bytes 884740
  38.9 12.6 %copy-start.1 = (bf16[32,1,1,2,2304]{4,3,2,1,0:T(2,128)(2,1)S(1)}, bf16[32,1,1,2,2304]{4,3,2,1,0:T(2,128)(2,1)}, u32[]{:S(2)}) copy-start(bf16[32,1,1,2,2304]{4,3,2,1,0:T(2,128)(2,1)} %param.9) | copy-start | bytes 884740
  41.0 23.9 %all-to-all-start.1 = ((bf16[32,2,4608]{2,1,0:T(2,128)(2,1)}), bf16[32,2,4608]{2,1,0:T(2,128)(2,1)S(1)}, u32[]{:S(2)}, u32[]{:S(2)}) async-start(bf16[32,2,4608]{2,1,0:T(2,128)(2,1)} %reshape.21), calls=%async_computation.1 | async-start | bytes 1179648 | tf_op jit(solution)/shard_map/all_to_all | solution.py:254

commit v2 on v1

--- a/solution.py
+++ b/solution.py
@@ -230,6 +230,7 @@
         out_shape=jax.ShapeDtypeStruct((2 * count, NYX), F32),
         in_specs=[vmem()] * 3,
         out_specs=vmem(),
+        compiler_params=pltpu.CompilerParams(vmem_limit_bytes=12 << 20),
         name="slab_part",
     )(planes.reshape(2 * count, NYX), potential, jnp.asarray(lateral_table()))
 
@@ -239,6 +240,7 @@
         in_specs=[smem()] * 2 + [vmem()] * 7,
         out_specs=vmem(),
         scratch_shapes=[pltpu.VMEM((NYX, LANES), F32)],
+        compiler_params=pltpu.CompilerParams(vmem_limit_bytes=12 << 20),
         name="owner_part",
     )(
         flags,
@@ -259,6 +261,7 @@
         out_shape=jax.ShapeDtypeStruct((2 * count, NYX), BF16),
         in_specs=[vmem()] * 2,
         out_specs=vmem(),
+        compiler_params=pltpu.CompilerParams(vmem_limit_bytes=12 << 20),
         name="join_part",
     )(base, returned.reshape(2 * count, 2 * NYX))
     return result.reshape(orbitals.shape)

time: 70.3 us -> 66.1 us (0.940); the launches traced: 69.8 us -> 64.9 us
  Pallas kernels: 10.7 us -> 4.67 us
  waiting for transfers between devices: 14.2 us -> 17.2 us
  local copies, waits for them, and re-layouts: 7.38 us -> 5.35 us
    all_to_all x1, waiting for transfers between devices: 8.99 us -> 12 us  [local(): lax.all_to_all(terms.reshape(count, 2, 2 * NYX), 'slab', split_axis=0, co...]
    pallas_call x1, Pallas kernels: 3.6 us -> 1.32 us  [local(): pl.pallas_call(slab_kernel, out_shape=jax.ShapeDtypeStruct((2 * count, NY...]
    pallas_call x1, Pallas kernels: 2.07 us -> 0.09 us  [local(): pl.pallas_call(final_kernel, out_shape=jax.ShapeDtypeStruct((2 * count, N...]
    pallas_call x1, Pallas kernels: 5.06 us -> 3.26 us  [local(): pl.pallas_call(owner_kernel, out_shape=jax.ShapeDtypeStruct((NZ, 2 * NYX)...]
    unnamed x10 -> x16, local copies, waits for them, and re-layouts: 1.45 us -> 3.03 us
    reshape x1, local copies, waits for them, and re-layouts: 2.16 us -> 1.04 us  [local(): terms.reshape(count, 2, 2 * NYX)]
    reshape x1, local copies, waits for them, and re-layouts: 1.79 us -> 0.83 us  [local(): return result.reshape(orbitals.shape)]
    reshape x1, local copies, waits for them, and re-layouts: 1.05 us -> 0.22 us  [local(): returned.reshape(2 * count, 2 * NYX)]
  transfers between devices with their start and end apart: 4 -> 4, of which waited for: 2 -> 2; matrix products, arithmetic and copies ran while one was open for 1% -> 0% of each run, Pallas kernels for 5% -> 2%
where the time goes in v2:
time: 66.1 us; the launch traced here: 64.9 us
  blocking collectives  23.2 us (35%)
  waiting for transfers between devices  17.2 us (26%)
  starting transfers between devices  14.4 us (22%)
  local copies, waits for them, and re-layouts  5.35 us (8%)
  Pallas kernels  4.67 us (7%)
    all_to_all x1, blocking collectives, local(): lax.all_to_all(planes, 'slab', split_axis=0, concat_axis=0, tiled=True)  23.2 us
    all_to_all x1, waiting for transfers between devices, local(): lax.all_to_all(terms.reshape(count, 2, 2 * NYX), 'slab', split_axis=0, co...  12 us
    all_to_all x1, starting transfers between devices, local(): lax.all_to_all(terms.reshape(count, 2, 2 * NYX), 'slab', split_axis=0, co...  10.4 us
    ppermute x1, waiting for transfers between devices, local(): ahead_flags = lax.ppermute(flags, chain, to_behind)  5.23 us
    pallas_call x1, Pallas kernels, local(): pl.pallas_call(owner_kernel, out_shape=jax.ShapeDtypeStruct((NZ, 2 * NYX)...  3.26 us
    unnamed x16, local copies, waits for them, and re-layouts  3.03 us
    ppermute x1, starting transfers between devices, local(): ahead = lax.ppermute(own, chain, to_behind)  2.3 us
    ppermute x1, starting transfers between devices, local(): behind = lax.ppermute(own, chain, to_ahead)  1.63 us
  transfers between devices with their start and end apart: 4, of which 2 were waited for; matrix products, arithmetic and copies ran while one was open for 0% of the time, Pallas kernels for 2%

profile of v2, /device:TPU:25, one launch (start us, length us, event | category | flops | bytes accessed | tf_op | source)
XLA Modules:
  0.0 64.9 jit_solution(7687329160417330846)
XLA Ops:
  0.0 23.2 %all_to_all.10 = bf16[32,2,2304]{2,1,0:T(2,128)(2,1)S(1)} all-to-all(bf16[32,2,2304]{2,1,0:T(2,128)(2,1)} %bitcast.5), channel_id=1, replica_groups=mesh['slab'=32,'orb'=8] {'slab'}, dimensions={0} | all-to-all | bytes 589824 | tf_op jit(solution)/shard_map/all_to_all | solution.py:223
  23.2 0.1 reshape.20.own
  23.3 2.3 %collective-permute-start.1 = (bf16[64,2304]{1,0:T(8,128)(2,1)S(1)}, bf16[64,2304]{1,0:T(8,128)(2,1)S(1)}, u32[]{:S(2)}, u32[]{:S(2)}) collective-permute-start(bf16[64,2304]{1,0:T(8,128)(2,1)S(1)} %reshape.20.own), channel_id=1, source_target_pairs={{1,0},{2,1},{3,2},{4,3},{5,4},{6,5},{7,6},{8,7},{9,8},{10,9},{11,1... | collective-permute-start | bytes 884744 | tf_op jit(solution)/shard_map/ppermute | solution.py:225
  25.6 1.6 %collective-permute-start.2 = (bf16[64,2304]{1,0:T(8,128)(2,1)S(1)}, bf16[64,2304]{1,0:T(8,128)(2,1)S(1)}, u32[]{:S(2)}, u32[]{:S(2)}) collective-permute-start(bf16[64,2304]{1,0:T(8,128)(2,1)S(1)} %reshape.20.own), channel_id=1, source_target_pairs={{0,1},{1,2},{2,3},{3,4},{4,5},{5,6},{6,7},{7,8},{8,9},{9,10},{10,1... | collective-permute-start | bytes 884744 | tf_op jit(solution)/shard_map/ppermute | solution.py:226
  27.2 0.0 collective-permute-start
  27.2 5.2 %collective-permute-done.ahead_flags = s32[1,2]{1,0:T(1,128)S(1)} collective-permute-done((s32[1,2]{1,0:T(1,128)}, s32[1,2]{1,0:T(1,128)S(1)}, u32[]{:S(2)}, u32[]{:S(2)}) %collective-permute-start) | collective-permute-done | bytes 40 | tf_op jit(solution)/shard_map/ppermute | solution.py:221
  32.5 0.0 collective-permute-done.1.ahead
  32.5 0.0 copy-start.2
  32.5 0.9 %copy-done.2 = bf16[256,256]{1,0:T(8,128)(2,1)S(1)} copy-done((bf16[256,256]{1,0:T(8,128)(2,1)S(1)}, bf16[256,256]{1,0:T(8,128)(2,1)}, u32[]{:S(2)}) %copy-start.2) | copy-done | bytes 131096
  33.4 0.7 %copy-done.3 = bf16[48,144]{1,0:T(8,128)(2,1)S(1)} copy-done((bf16[48,144]{1,0:T(8,128)(2,1)S(1)}, bf16[48,144]{1,0:T(8,128)(2,1)}, u32[]{:S(2)}) %copy-start.3) | copy-done | bytes 13848
  34.1 0.7 %copy-done.5 = bf16[64,128]{1,0:T(8,128)(2,1)S(1)} copy-done((bf16[64,128]{1,0:T(8,128)(2,1)S(1)}, bf16[64,128]{1,0:T(8,128)(2,1)}, u32[]{:S(2)}) %copy-start.5) | copy-done | bytes 16408
  34.8 0.7 %copy-done.6 = s32[1,1,1,2]{3,2,1,0:T(1,128)S(1)} copy-done((s32[1,1,1,2]{3,2,1,0:T(1,128)S(1)}, s32[1,1,1,2]{3,2,1,0:T(1,128)}, u32[]{:S(2)}) %copy-start.6) | copy-done | bytes 32
  35.5 3.3 %owner_part.1 = bf16[64,4608]{1,0:T(8,128)(2,1)S(1)} custom-call(s32[1,2]{1,0:T(1,128)S(1)} %bitcast.4, s32[1,2]{1,0:T(1,128)S(1)} %collective-permute-done.ahead_flags, bf16[64,2304]{1,0:T(8,128)(2,1)S(1)} %reshape.20.own, bf16[64,2304]{1,0:T(8,128)(2,1)S(1)} %collective-permute-done.1.ahead, bf16[64,2304]{1,0:T(8,128)(2,1)S(1)} %collective-permute-done.2.behind, ...), custom_call_target="tpu_custom_call" | custom-call | tf_op jit(solution)/shard_map/owner_part/pallas_call | solution.py:237
  38.8 0.0 copy-start.7
  38.8 0.0 copy-start
  38.8 0.0 copy-start.4
  38.8 1.0 %reshape.21 = bf16[32,2,4608]{2,1,0:T(2,128)(2,1)} reshape(bf16[64,4608]{1,0:T(8,128)(2,1)S(1)} %owner_part.1) | data formatting | bytes 1179648 | tf_op jit(solution)/shard_map/reshape | solution.py:257
  39.8 10.4 %all-to-all-start.1 = ((bf16[32,2,4608]{2,1,0:T(2,128)(2,1)}), bf16[32,2,4608]{2,1,0:T(2,128)(2,1)S(1)}, u32[]{:S(2)}, u32[]{:S(2)}) async-start(bf16[32,2,4608]{2,1,0:T(2,128)(2,1)} %reshape.21), calls=%async_computation.1 | async-start | bytes 1179648 | tf_op jit(solution)/shard_map/all_to_all | solution.py:256
  50.3 0.1 reshape_reshape.3.planes
  50.4 1.3 %slab_part.1.base = f32[64,2304]{1,0:T(8,128)S(1)} custom-call(bf16[64,2304]{1,0:T(8,128)(2,1)S(1)} %reshape_reshape.3.planes, f32[2,2304]{1,0:T(2,128)S(1)} %copy-done.4, bf16[1792,384]{1,0:T(8,128)(2,1)S(1)} %copy-done), custom_call_target="tpu_custom_call" | custom-call | tf_op jit(solution)/shard_map/slab_part/pallas_call | solution.py:228
  51.8 12.0 %all-to-all-done.1 = bf16[32,2,4608]{2,1,0:T(2,128)(2,1)S(1)} async-done(((bf16[32,2,4608]{2,1,0:T(2,128)(2,1)}), bf16[32,2,4608]{2,1,0:T(2,128)(2,1)S(1)}, u32[]{:S(2)}, u32[]{:S(2)}) %all-to-all-start.1) | async-done | bytes 589856 | tf_op jit(solution)/shard_map/all_to_all | solution.py:256
  63.7 0.2 reshape.22.returned
  63.9 0.1 join_part.1
  64.0 0.8 %reshape.23 = bf16[32,1,1,2,2304]{4,3,0,2,1:T(2,128)(2,1)} reshape(bf16[64,2304]{1,0:T(8,128)(2,1)S(1)} %join_part.1) | data formatting | bytes 589824 | tf_op jit(solution)/shard_map/reshape | solution.py:267
  (9 shorter events, 0.0 us)
Async XLA Ops:
  0.0 32.5 %copy-start.1 = (f32[2304,128]{1,0:T(8,128)S(1)}, f32[2304,128]{1,0:T(8,128)}, u32[]{:S(2)}) copy-start(f32[2304,128]{1,0:T(8,128)} %constant.13.clone.wave_t) | copy-start | bytes 3538948
  23.3 9.2 %collective-permute-start.1 = (bf16[64,2304]{1,0:T(8,128)(2,1)S(1)}, bf16[64,2304]{1,0:T(8,128)(2,1)S(1)}, u32[]{:S(2)}, u32[]{:S(2)}) collective-permute-start(bf16[64,2304]{1,0:T(8,128)(2,1)S(1)} %reshape.20.own), channel_id=1, source_target_pairs={{1,0},{2,1},{3,2},{4,3},{5,4},{6,5},{7,6},{8,7},{9,8},{10,9},{11,1... | collective-permute-start | bytes 884744 | tf_op jit(solution)/shard_map/ppermute | solution.py:225
  25.6 6.9 %collective-permute-start.2 = (bf16[64,2304]{1,0:T(8,128)(2,1)S(1)}, bf16[64,2304]{1,0:T(8,128)(2,1)S(1)}, u32[]{:S(2)}, u32[]{:S(2)}) collective-permute-start(bf16[64,2304]{1,0:T(8,128)(2,1)S(1)} %reshape.20.own), channel_id=1, source_target_pairs={{0,1},{1,2},{2,3},{3,4},{4,5},{5,6},{6,7},{7,8},{8,9},{9,10},{10,1... | collective-permute-start | bytes 884744 | tf_op jit(solution)/shard_map/ppermute | solution.py:226
  27.2 5.2 %collective-permute-start = (s32[1,2]{1,0:T(1,128)}, s32[1,2]{1,0:T(1,128)S(1)}, u32[]{:S(2)}, u32[]{:S(2)}) collective-permute-start(s32[1,2]{1,0:T(1,128)} %bitcast.3), channel_id=1, source_target_pairs={{1,0},{2,1},{3,2},{4,3},{5,4},{6,5},{7,6},{8,7},{9,8},{10,9},{11,1... | collective-permute-start | bytes 32 | tf_op jit(solution)/shard_map/ppermute | solution.py:221
  32.5 0.9 %copy-start.2 = (bf16[256,256]{1,0:T(8,128)(2,1)S(1)}, bf16[256,256]{1,0:T(8,128)(2,1)}, u32[]{:S(2)}) copy-start(bf16[256,256]{1,0:T(8,128)(2,1)} %constant.11.clone.depth_t) | copy-start | bytes 393220
  33.4 0.7 %copy-start.3 = (bf16[48,144]{1,0:T(8,128)(2,1)S(1)}, bf16[48,144]{1,0:T(8,128)(2,1)}, u32[]{:S(2)}) copy-start(bf16[48,144]{1,0:T(8,128)(2,1)} %constant.12.clone.side_t) | copy-start | bytes 41476
  34.1 0.7 %copy-start.5 = (bf16[64,128]{1,0:T(8,128)(2,1)S(1)}, bf16[64,128]{1,0:T(8,128)(2,1)}, u32[]{:S(2)}) copy-start(bf16[64,128]{1,0:T(8,128)(2,1)} %constant.14.clone.vert_t) | copy-start | bytes 49156
  34.8 0.7 %copy-start.6 = (s32[1,1,1,2]{3,2,1,0:T(1,128)S(1)}, s32[1,1,1,2]{3,2,1,0:T(1,128)}, u32[]{:S(2)}) copy-start(s32[1,1,1,2]{3,2,1,0:T(1,128)} %param.11) | copy-start | bytes 28
  38.8 11.5 %copy-start.7 = (bf16[32,1,1,2,2304]{4,3,2,1,0:T(2,128)(2,1)S(1)}, bf16[32,1,1,2,2304]{4,3,2,1,0:T(2,128)(2,1)}, u32[]{:S(2)}) copy-start(bf16[32,1,1,2,2304]{4,3,2,1,0:T(2,128)(2,1)} %param.9) | copy-start | bytes 884740
  38.8 11.6 %copy-start = (bf16[1792,384]{1,0:T(8,128)(2,1)S(1)}, bf16[1792,384]{1,0:T(8,128)(2,1)}, u32[]{:S(2)}) copy-start(bf16[1792,384]{1,0:T(8,128)(2,1)} %constant.10.clone.lateral_t) | copy-start | bytes 4128772
  38.8 11.6 %copy-start.4 = (f32[2,2304]{1,0:T(2,128)S(1)}, f32[2,2304]{1,0:T(2,128)}, u32[]{:S(2)}) copy-start(f32[2,2304]{1,0:T(2,128)} %potential.1) | copy-start | bytes 55300
  39.8 23.9 %all-to-all-start.1 = ((bf16[32,2,4608]{2,1,0:T(2,128)(2,1)}), bf16[32,2,4608]{2,1,0:T(2,128)(2,1)S(1)}, u32[]{:S(2)}, u32[]{:S(2)}) async-start(bf16[32,2,4608]{2,1,0:T(2,128)(2,1)} %reshape.21), calls=%async_computation.1 | async-start | bytes 1179648 | tf_op jit(solution)/shard_map/all_to_all | solution.py:256

commit v3 on v1

--- a/solution.py
+++ b/solution.py
@@ -17,6 +17,13 @@
 GROUP = 384
 REACH_LANES = 256
 WINDOW = GROUP + 2 * REACH_LANES
+DEPTH_AT = NYX
+SIDE_AT = DEPTH_AT + 512
+VERT_AT = SIDE_AT + 2 * NX
+
+CODE_RANGE = 255.0
+CODE_SLOPE = 31.0
+CODE_SHIFT = 124.0
 
 stencil_weights = (-205.0 / 72.0, 8.0 / 5.0, -1.0 / 5.0, 8.0 / 315.0, -1.0 / 560.0)
 screening = 0.11
@@ -84,6 +91,23 @@
 def vertical_table():
     high, low = split_table(-0.5 * second_difference(NZ))
     return np.concatenate([high, low], axis=1)
+
+
+def owner_tables():
+    depth = depth_table().astype(np.float32)
+    side = np.zeros((NX, 2 * LANES), np.float32)
+    side[:, : 3 * NX] = side_table().astype(np.float32)
+    return np.concatenate(
+        [
+            kernel_table(),
+            depth[:, :LANES],
+            depth[:, LANES:],
+            side[:, :LANES],
+            side[:, LANES:],
+            vertical_table().astype(np.float32),
+        ],
+        axis=0,
+    )
 
 
 def lateral_table():
@@ -123,19 +147,23 @@
 
 
 def owner_kernel(
-    flags, ahead_flags, own, ahead, behind, depth_t, side_t, wave_t, vert_t, out, work
+    flags_hbm, ahead_flags, own, mate, far, tables, out, work, term_work, flags, flags_done
 ):
-    w_ahead = (flags[0, 0] + ahead_flags[0, 1]).astype(F32) * (-mixing)
-    w_behind = (flags[0, 1] + 1).astype(F32) * (-mixing)
-    depth = depth_t[...]
-    side = side_t[...]
-    vert = vert_t[...]
+    flags_copy = pltpu.make_async_copy(flags_hbm, flags, flags_done)
+    flags_copy.start()
+    depth = jnp.concatenate(
+        [tables[DEPTH_AT : DEPTH_AT + 256, :], tables[DEPTH_AT + 256 : SIDE_AT, :]], axis=1
+    ).astype(BF16)
+    side = jnp.concatenate(
+        [tables[SIDE_AT : SIDE_AT + NX, :], tables[SIDE_AT + NX : VERT_AT, :]], axis=1
+    )[:, : 3 * NX].astype(BF16)
+    vert = tables[VERT_AT : VERT_AT + NZ, :].astype(BF16)
 
     for chunk in range(CHUNKS):
         cols = slice(chunk * LANES, (chunk + 1) * LANES)
         mine = own[:, cols].astype(F32)
         density = jnp.concatenate(
-            [mine * ahead[:, cols].astype(F32), mine * behind[:, cols].astype(F32)], axis=0
+            [mine * mate[:, cols].astype(F32), mine * far[:, cols].astype(F32)], axis=0
         )
         work[cols, :] = depth_turn(density.T, depth)
 
@@ -154,8 +182,8 @@
         turned = side_turn(jnp.concatenate([work[first, :], work[second, :]], axis=1), side)
         factor = jnp.concatenate(
             [
-                wave_t[2 * step * NY : (2 * step + 1) * NY, :],
-                wave_t[(2 * step + 1) * NY : (2 * step + 2) * NY, :],
+                tables[2 * step * NY : (2 * step + 1) * NY, :],
+                tables[(2 * step + 1) * NY : (2 * step + 2) * NY, :],
             ],
             axis=1,
         )
@@ -165,19 +193,35 @@
     for step in range(NY // 2):
         along_x(step)
 
+    flags_copy.wait()
+    w_ahead = (flags[0, 0] + ahead_flags[0, 1]).astype(F32) * (-mixing)
+    w_behind = (flags[0, 1] + 1).astype(F32) * (-mixing)
+    even = lax.axis_index("orb") % 2 == 0
+    w_mate = jnp.where(even, w_ahead, w_behind)
+    w_far = jnp.where(even, w_behind, w_ahead)
+    peak = jnp.zeros((NZ, LANES), F32)
     for chunk in range(CHUNKS):
         cols = slice(chunk * LANES, (chunk + 1) * LANES)
         pots = depth_turn(work[cols, :], depth).T
         mine = own[:, cols]
         term = jnp.dot(vert, jnp.concatenate([mine, mine], axis=0), preferred_element_type=F32)
-        term = term + w_ahead * (pots[:NZ] * ahead[:, cols].astype(F32))
-        term = term + w_behind * (pots[NZ:] * behind[:, cols].astype(F32))
-        high, low = halves(term)
-        out[:, cols] = high
-        out[:, NYX + chunk * LANES : NYX + (chunk + 1) * LANES] = low
-
-
-def slab_kernel(planes, potential, lateral_t, out):
+        term = term + w_mate * (pots[:NZ] * mate[:, cols].astype(F32))
+        term = term + w_far * (pots[NZ:] * far[:, cols].astype(F32))
+        term_work[:, cols] = term
+        peak = jnp.maximum(peak, jnp.abs(term))
+    top = jnp.max(jnp.max(peak, axis=0, keepdims=True), axis=1, keepdims=True)
+    scale = jnp.broadcast_to(jnp.maximum(top * 1.02, 1e-30), (NZ, LANES)).astype(BF16)
+    out[:, NYX:] = scale
+    inverse = CODE_RANGE / scale.astype(F32)
+    for chunk in range(CHUNKS):
+        cols = slice(chunk * LANES, (chunk + 1) * LANES)
+        term = term_work[:, cols]
+        code = jnp.exp2(jnp.log2(1.0 + jnp.abs(term) * inverse) * CODE_SLOPE - CODE_SHIFT)
+        out[:, cols] = jnp.where(term < 0, -code, code).astype(BF16)
+
+
+def slab_kernel(planes, potential, lateral_t, tables, own, out, tables_out):
+    del tables, own, tables_out
     rows = planes.shape[0]
     parity = lax.broadcasted_iota(jnp.int32, (8, GROUP), 0) % 2
     for start in range(0, NYX, GROUP):
@@ -198,9 +242,13 @@
 
 
 def final_kernel(base, returned, out):
-    out[...] = (
-        base[...] + returned[:, :NYX].astype(F32) + returned[:, NYX:].astype(F32)
-    ).astype(BF16)
+    scale = returned[:, NYX:].astype(F32) * (1.0 / CODE_RANGE)
+    for chunk in range(CHUNKS):
+        cols = slice(chunk * LANES, (chunk + 1) * LANES)
+        code = returned[:, cols].astype(F32)
+        size = jnp.exp2((jnp.log2(jnp.abs(code)) + CODE_SHIFT) * (1.0 / CODE_SLOPE)) - 1.0
+        term = jnp.where(code < 0, -size, size) * scale
+        out[:, cols] = (base[:, cols] + term).astype(BF16)
 
 
 def vmem():
@@ -214,53 +262,59 @@
 def local(orbitals, potential, partners, pair_valid):
     count = lax.axis_size("slab")
     total = count * lax.axis_size("orb")
+    chain = ("slab", "orb")
     to_behind = [((i + 1) % total, i) for i in range(total)]
-    to_ahead = [(i, (i + 1) % total) for i in range(total)]
-    chain = ("slab", "orb")
+    to_mate = [(i, i ^ 1) for i in range(total)]
+    to_far = [(i, (i + 2 * (i % 2) - 1) % total) for i in range(total)]
     flags = pair_valid.reshape(1, 2)
     ahead_flags = lax.ppermute(flags, chain, to_behind)
     planes = orbitals.reshape(count, 2, NYX)
     own = lax.all_to_all(planes, "slab", split_axis=0, concat_axis=0, tiled=True)
     own = own.reshape(NZ, NYX)
-    ahead = lax.ppermute(own, chain, to_behind)
-    behind = lax.ppermute(own, chain, to_ahead)
-
-    base = pl.pallas_call(
+    far = lax.ppermute(own, chain, to_far)
+    mate = lax.ppermute(own, chain, to_mate)
+    limits = pltpu.CompilerParams(vmem_limit_bytes=12 << 20)
+
+    tables = jnp.asarray(owner_tables())
+    base, tables = pl.pallas_call(
         slab_kernel,
-        out_shape=jax.ShapeDtypeStruct((2 * count, NYX), F32),
-        in_specs=[vmem()] * 3,
-        out_specs=vmem(),
+        out_shape=(
+            jax.ShapeDtypeStruct((2 * count, NYX), F32),
+            jax.ShapeDtypeStruct(tables.shape, F32),
+        ),
+        in_specs=[vmem()] * 4 + [pl.BlockSpec(memory_space=pl.ANY)],
+        out_specs=(vmem(), vmem()),
+        input_output_aliases={3: 1},
+        compiler_params=limits,
         name="slab_part",
-    )(planes.reshape(2 * count, NYX), potential, jnp.asarray(lateral_table()))
-
+    )(planes.reshape(2 * count, NYX), potential, jnp.asarray(lateral_table()), tables, own)
+
+    wide = NYX + LANES
     terms = pl.pallas_call(
         owner_kernel,
-        out_shape=jax.ShapeDtypeStruct((NZ, 2 * NYX), BF16),
-        in_specs=[smem()] * 2 + [vmem()] * 7,
+        out_shape=jax.ShapeDtypeStruct((NZ, wide), BF16),
+        in_specs=[pl.BlockSpec(memory_space=pltpu.HBM), smem()] + [vmem()] * 4,
         out_specs=vmem(),
-        scratch_shapes=[pltpu.VMEM((NYX, LANES), F32)],
+        scratch_shapes=[
+            pltpu.VMEM((NYX, LANES), F32),
+            pltpu.VMEM((NZ, NYX), F32),
+            pltpu.SMEM((1, 2), jnp.int32),
+            pltpu.SemaphoreType.DMA,
+        ],
+        compiler_params=limits,
         name="owner_part",
-    )(
-        flags,
-        ahead_flags,
-        own,
-        ahead,
-        behind,
-        jnp.asarray(depth_table()),
-        jnp.asarray(side_table()),
-        jnp.asarray(kernel_table()),
-        jnp.asarray(vertical_table()),
-    )
+    )(flags, ahead_flags, own, mate, far, tables)
     returned = lax.all_to_all(
-        terms.reshape(count, 2, 2 * NYX), "slab", split_axis=0, concat_axis=0, tiled=True
+        terms.reshape(count, 2, wide), "slab", split_axis=0, concat_axis=0, tiled=True
     )
     result = pl.pallas_call(
         final_kernel,
         out_shape=jax.ShapeDtypeStruct((2 * count, NYX), BF16),
         in_specs=[vmem()] * 2,
         out_specs=vmem(),
+        compiler_params=limits,
         name="join_part",
-    )(base, returned.reshape(2 * count, 2 * NYX))
+    )(base, returned.reshape(2 * count, wide))
     return result.reshape(orbitals.shape)
 
 

time: 70.3 us -> 56.8 us (0.81)
  blocking collectives: 23 us -> 40.8 us
  starting transfers between devices: 14.4 us -> 3.17 us
  waiting for transfers between devices: 14.2 us -> 3.69 us
  Pallas kernels: 10.7 us -> 5.32 us
  local copies, waits for them, and re-layouts: 7.38 us -> 3.57 us
    all_to_all x0 -> x1, blocking collectives: none -> 17.6 us  [local(): lax.all_to_all(terms.reshape(count, 2, wide), 'slab', split_axis=0, conca...]
    all_to_all x1 -> x0, starting transfers between devices: 10.4 us -> none  [local(): lax.all_to_all(terms.reshape(count, 2, 2 * NYX), 'slab', split_axis=0, co...]
    all_to_all x1 -> x0, waiting for transfers between devices: 8.99 us -> none  [local(): lax.all_to_all(terms.reshape(count, 2, 2 * NYX), 'slab', split_axis=0, co...]
    pallas_call x2, Pallas kernels: 8.66 us -> 5.05 us  [the longest x1 3.69 us: local(): pl.pallas_call(owner_kernel, out_shape=jax.ShapeDtypeStruct((NZ, wide), B...]
    reshape x2, local copies, waits for them, and re-layouts: 3.2 us -> 0.24 us  [the longest x1 0.12 us: local(): terms.reshape(count, 2, wide)]
    pallas_call x1, Pallas kernels: 2.07 us -> 0.26 us  [local(): pl.pallas_call(final_kernel, out_shape=jax.ShapeDtypeStruct((2 * count, N...]
    ppermute x2, starting transfers between devices: 3.93 us -> 2.32 us  [the longest x1 2.31 us: local(): mate = lax.ppermute(own, chain, to_mate)]
    ppermute x1, waiting for transfers between devices: 5.23 us -> 3.68 us  [local(): ahead_flags = lax.ppermute(flags, chain, to_behind)]
  transfers between devices with their start and end apart: 4 -> 3, of which waited for: 2 -> 1; matrix products, arithmetic and copies ran while one was open for 1% -> 2% of each run, Pallas kernels for 5% -> 2%
where the time goes in v3:
time: 56.8 us; the launch traced here: 56.6 us
  blocking collectives  40.8 us (72%)
  Pallas kernels  5.32 us (9%)
  waiting for transfers between devices  3.69 us (6%)
  local copies, waits for them, and re-layouts  3.57 us (6%)
  starting transfers between devices  3.17 us (6%)
    all_to_all x1, blocking collectives, local(): lax.all_to_all(planes, 'slab', split_axis=0, concat_axis=0, tiled=True)  23.2 us
    all_to_all x1, blocking collectives, local(): lax.all_to_all(terms.reshape(count, 2, wide), 'slab', split_axis=0, conca...  17.6 us
    pallas_call x1, Pallas kernels, local(): pl.pallas_call(owner_kernel, out_shape=jax.ShapeDtypeStruct((NZ, wide), B...  3.69 us
    ppermute x1, waiting for transfers between devices, local(): ahead_flags = lax.ppermute(flags, chain, to_behind)  3.68 us
    ppermute x1, starting transfers between devices, local(): mate = lax.ppermute(own, chain, to_mate)  2.31 us
    pallas_call x1, Pallas kernels, local(): pl.pallas_call(slab_kernel, out_shape=(jax.ShapeDtypeStruct((2 * count, N...  1.37 us
    unnamed x9, local copies, waits for them, and re-layouts  1.33 us
  transfers between devices with their start and end apart: 3, of which 1 were waited for; matrix products, arithmetic and copies ran while one was open for 2% of the time, Pallas kernels for 2%

profile of v3, /device:TPU:25, one launch (start us, length us, event | category | flops | bytes accessed | tf_op | source)
XLA Modules:
  0.0 56.6 jit_solution(2109940467238350544)
XLA Ops:
  0.0 0.0 copy-start.3
  0.0 23.2 %all_to_all.10 = bf16[32,2,2304]{2,1,0:T(2,128)(2,1)S(1)} all-to-all(bf16[32,2,2304]{2,1,0:T(2,128)(2,1)} %bitcast.5), channel_id=1, replica_groups=mesh['slab'=32,'orb'=8] {'slab'}, dimensions={0} | all-to-all | bytes 589824 | tf_op jit(solution)/shard_map/all_to_all | solution.py:272
  23.2 0.1 reshape.19.own
  23.3 2.3 %collective-permute-start.1 = (bf16[64,2304]{1,0:T(8,128)(2,1)S(1)}, bf16[64,2304]{1,0:T(8,128)(2,1)S(1)}, u32[]{:S(2)}, u32[]{:S(2)}) collective-permute-start(bf16[64,2304]{1,0:T(8,128)(2,1)S(1)} %reshape.19.own), channel_id=1, source_target_pairs={{0,1},{1,0},{2,3},{3,2},{4,5},{5,4},{6,7},{7,6},{8,9},{9,8},{10,11... | collective-permute-start | bytes 884744 | tf_op jit(solution)/shard_map/ppermute | solution.py:275
  25.6 0.0 collective-permute-start.2
  25.6 0.9 %collective-permute-start = (s32[1,2]{1,0:T(1,128)}, s32[1,2]{1,0:T(1,128)S(1)}, u32[]{:S(2)}, u32[]{:S(2)}) collective-permute-start(s32[1,2]{1,0:T(1,128)} %bitcast.3), channel_id=1, source_target_pairs={{1,0},{2,1},{3,2},{4,3},{5,4},{6,5},{7,6},{8,7},{9,8},{10,9},{11,1... | collective-permute-start | bytes 32 | tf_op jit(solution)/shard_map/ppermute | solution.py:270
  26.5 1.1 %reshape_reshape.3.planes = bf16[64,2304]{1,0:T(8,128)(2,1)S(1)} reshape(bf16[32,1,1,2,2304]{4,3,2,1,0:T(2,128)(2,1)} %param.6) | data formatting | bytes 589824 | tf_op jit(solution)/shard_map/reshape;reshape | solution.py:290
  27.5 0.0 copy-done.3
  27.6 0.0 copy-start
  27.6 0.0 copy-start.1
  27.6 0.1 copy.10.tables
  27.7 1.2 %copy-done = bf16[1792,384]{1,0:T(8,128)(2,1)S(1)} copy-done((bf16[1792,384]{1,0:T(8,128)(2,1)S(1)}, bf16[1792,384]{1,0:T(8,128)(2,1)}, u32[]{:S(2)}) %copy-start) | copy-done | bytes 1376280
  28.9 0.0 copy-done.1
  28.9 1.4 %slab_part.1 = (f32[64,2304]{1,0:T(8,128)S(1)}, f32[2976,128]{1,0:T(8,128)S(1)}) custom-call(bf16[64,2304]{1,0:T(8,128)(2,1)S(1)} %reshape_reshape.3.planes, f32[2,2304]{1,0:T(2,128)S(1)} %copy-done.1, bf16[1792,384]{1,0:T(8,128)(2,1)S(1)} %copy-done, f32[2976,128]{1,0:T(8,128)S(1)} %copy.10.tables, ...), custom_call_target="tpu_custom_call", output_to_operand_aliasing={{1}: (3, {})} | custom-call | tf_op jit(solution)/shard_map/slab_part/pallas_call | solution.py:279
  30.3 3.7 %collective-permute-done.ahead_flags = s32[1,2]{1,0:T(1,128)S(1)} collective-permute-done((s32[1,2]{1,0:T(1,128)}, s32[1,2]{1,0:T(1,128)S(1)}, u32[]{:S(2)}, u32[]{:S(2)}) %collective-permute-start) | collective-permute-done | bytes 40 | tf_op jit(solution)/shard_map/ppermute | solution.py:270
  34.0 0.0 collective-permute-done.1.mate
  34.0 0.0 collective-permute-done.2.far
  34.0 0.0 copy-done.2
  34.0 3.7 %owner_part.1 = bf16[64,2432]{1,0:T(8,128)(2,1)S(1)} custom-call(s32[1,2]{1,0:T(1,128)S(1)} %bitcast.4, s32[1,2]{1,0:T(1,128)S(1)} %collective-permute-done.ahead_flags, bf16[64,2304]{1,0:T(8,128)(2,1)S(1)} %reshape.19.own, bf16[64,2304]{1,0:T(8,128)(2,1)S(1)} %collective-permute-done.1.mate, bf16[64,2304]{1,0:T(8,128)(2,1)S(1)} %collective-permute-done.2.far, ...), custom_call_target="tpu_custom_call" | custom-call | tf_op jit(solution)/shard_map/owner_part/pallas_call | solution.py:293
  37.7 0.1 reshape.21
  37.8 17.6 %all_to_all.11 = bf16[32,2,2432]{2,1,0:T(2,128)(2,1)S(1)} all-to-all(bf16[32,2,2432]{2,1,0:T(2,128)(2,1)S(1)} %reshape.21), channel_id=1, replica_groups=mesh['slab'=32,'orb'=8] {'slab'}, dimensions={0} | all-to-all | bytes 622592 | tf_op jit(solution)/shard_map/all_to_all | solution.py:307
  55.4 0.1 reshape.22.returned
  55.5 0.3 join_part.1
  55.8 0.8 %reshape.23 = bf16[32,1,1,2,2304]{4,3,0,2,1:T(2,128)(2,1)} reshape(bf16[64,2304]{1,0:T(8,128)(2,1)S(1)} %join_part.1) | data formatting | bytes 589824 | tf_op jit(solution)/shard_map/reshape | solution.py:318
  (1 shorter events, 0.0 us)
Async XLA Ops:
  0.0 27.5 %copy-start.3 = (f32[2976,128]{1,0:T(8,128)S(1)}, f32[2976,128]{1,0:T(8,128)}, u32[]{:S(2)}) copy-start(f32[2976,128]{1,0:T(8,128)} %constant.4.clone) | copy-start | bytes 4571140
  23.3 10.7 %collective-permute-start.1 = (bf16[64,2304]{1,0:T(8,128)(2,1)S(1)}, bf16[64,2304]{1,0:T(8,128)(2,1)S(1)}, u32[]{:S(2)}, u32[]{:S(2)}) collective-permute-start(bf16[64,2304]{1,0:T(8,128)(2,1)S(1)} %reshape.19.own), channel_id=1, source_target_pairs={{0,1},{1,0},{2,3},{3,2},{4,5},{5,4},{6,7},{7,6},{8,9},{9,8},{10,11... | collective-permute-start | bytes 884744 | tf_op jit(solution)/shard_map/ppermute | solution.py:275
  25.6 8.4 %collective-permute-start.2 = (bf16[64,2304]{1,0:T(8,128)(2,1)S(1)}, bf16[64,2304]{1,0:T(8,128)(2,1)S(1)}, u32[]{:S(2)}, u32[]{:S(2)}) collective-permute-start(bf16[64,2304]{1,0:T(8,128)(2,1)S(1)} %reshape.19.own), channel_id=1, source_target_pairs={{0,255},{1,2},{2,1},{3,4},{4,3},{5,6},{6,5},{7,8},{8,7},{9,10},{10... | collective-permute-start | bytes 884744 | tf_op jit(solution)/shard_map/ppermute | solution.py:274
  25.6 8.3 %collective-permute-start = (s32[1,2]{1,0:T(1,128)}, s32[1,2]{1,0:T(1,128)S(1)}, u32[]{:S(2)}, u32[]{:S(2)}) collective-permute-start(s32[1,2]{1,0:T(1,128)} %bitcast.3), channel_id=1, source_target_pairs={{1,0},{2,1},{3,2},{4,3},{5,4},{6,5},{7,6},{8,7},{9,8},{10,9},{11,1... | collective-permute-start | bytes 32 | tf_op jit(solution)/shard_map/ppermute | solution.py:270
  27.6 1.3 %copy-start = (bf16[1792,384]{1,0:T(8,128)(2,1)S(1)}, bf16[1792,384]{1,0:T(8,128)(2,1)}, u32[]{:S(2)}) copy-start(bf16[1792,384]{1,0:T(8,128)(2,1)} %constant.5.clone.lateral_t) | copy-start | bytes 4128772
  27.6 1.3 %copy-start.1 = (f32[2,2304]{1,0:T(2,128)S(1)}, f32[2,2304]{1,0:T(2,128)}, u32[]{:S(2)}) copy-start(f32[2,2304]{1,0:T(2,128)} %potential.1) | copy-start | bytes 55300
  28.9 5.1 %copy-start.2 = (s32[1,1,1,2]{3,2,1,0:T(1,128)S(1)}, s32[1,1,1,2]{3,2,1,0:T(1,128)}, u32[]{:S(2)}) copy-start(s32[1,1,1,2]{3,2,1,0:T(1,128)} %param.8) | copy-start | bytes 28
